TPU v7x, 32 devices: a whole 2x2x4 slice. The times are simulated.
32 devices in a mesh: row: 4 (over x, core), col: 8 (over z, y).
Axes of the slice: x: 2, y: 2, z: 4, core: 2. Of those that a mesh axis runs over, the one named last changes fastest.
Arguments:
- pair: bfloat16 [768, 768, 512], P('row', 'col'), may hold values from -6 to 6
- w_bias: bfloat16 [512, 96], replicated, may hold values from -0.25 to 0.25
- queries: bfloat16 [768, 1536], P('row', 'col'), may hold values from -360 to 360
- keys: bfloat16 [768, 1536], P('col', 'row'), may hold values from -6 to 6
- values: bfloat16 [768, 1536], P('col', 'row'), may hold values from -6 to 6
- d_out: bfloat16 [768, 1536], P('row', 'col'), may hold values from -6 to 6
Outputs:
- d_pair: bfloat16 [768, 768, 512], P('row', 'col')
- d_wbias: float32 [512, 96], replicated
- d_queries: bfloat16 [768, 1536], P('row', 'col')
- d_keys: bfloat16 [768, 1536], P('col', 'row')
- d_values: bfloat16 [768, 1536], P('col', 'row')
All inputs are finite; a program needn't handle non-finite values.
Results may differ from a plain program's by a relative error of at most 0.0095.
Values may be sent and summed in bfloat16 or wider, within the bound.
A program may use at most 128 MiB of HBM per device.

v0:
```python
import jax
import jax.numpy as jnp
from jax import lax
from jax.sharding import PartitionSpec as P

D = 1536
H = 96
P_SIZE = 512
HD = 16


def joined(value, axis, join):
    pieces = jax.tree.map(lambda part: lax.all_gather(part, axis), value)
    head = jax.tree.map(lambda part: part[0], pieces)
    tail = jax.tree.map(lambda part: part[1:], pieces)
    subtotal, _ = lax.scan(lambda subtotal, piece: (join(subtotal, piece), None), head, tail)
    return subtotal


def combine_stats(former, latter):
    joined_max = jnp.maximum(former[0], latter[0])
    scale_former = jnp.exp(former[0] - joined_max)
    scale_latter = jnp.exp(latter[0] - joined_max)
    return (
        joined_max,
        former[1] * scale_former + latter[1] * scale_latter,
        former[2] * scale_former + latter[2] * scale_latter,
    )


def on_device(pair, w_bias, queries, keys, values, d_out):
    row_count = pair.shape[0]
    col_count = pair.shape[1]
    query_full, out_full = (
        lax.all_gather(queries, "col", axis=1, tiled=True),
        lax.all_gather(d_out, "col", axis=1, tiled=True),
    )
    key_full, value_full = (
        lax.all_gather(keys, "row", axis=1, tiled=True),
        lax.all_gather(values, "row", axis=1, tiled=True),
    )
    query_heads = query_full.reshape(row_count, H, HD)
    out_heads = out_full.reshape(row_count, H, HD)
    key_heads = key_full.reshape(col_count, H, HD)
    value_heads = value_full.reshape(col_count, H, HD)
    flat_pair = pair.reshape(row_count * col_count, P_SIZE)
    pair_bias = jnp.dot(flat_pair, w_bias, preferred_element_type=jnp.float32).reshape(
        row_count, col_count, H
    )
    scale = 1.0 / HD**0.5
    scores = jnp.einsum(
        "ihd,jhd->hij", query_heads, key_heads, preferred_element_type=jnp.float32
    ) * scale + pair_bias.transpose(2, 0, 1)
    grad_prob = jnp.einsum(
        "ihd,jhd->hij", out_heads, value_heads, preferred_element_type=jnp.float32
    )
    local_max = jnp.max(scores, axis=-1)
    exp_scores = jnp.exp(scores - local_max[..., None])
    local_stats = (
        local_max,
        jnp.sum(exp_scores, axis=-1),
        jnp.sum(exp_scores * grad_prob, axis=-1),
    )
    row_max, row_total, row_upper = joined(local_stats, "col", combine_stats)
    weights = jnp.exp(scores - row_max[..., None]) / row_total[..., None]
    row_delta = row_upper / row_total
    grad_score = (weights * (grad_prob - row_delta[..., None])).astype(jnp.bfloat16)
    weights_low = weights.astype(jnp.bfloat16)
    score_flat = grad_score.transpose(1, 2, 0).reshape(row_count * col_count, H)
    d_pair = (
        jnp.dot(score_flat, w_bias.T, preferred_element_type=jnp.float32)
        .astype(jnp.bfloat16)
        .reshape(row_count, col_count, P_SIZE)
    )
    weight_term = jnp.dot(flat_pair.T, score_flat, preferred_element_type=jnp.float32)
    d_wbias = lax.psum(weight_term, ("row", "col"))
    query_term = (
        jnp.einsum("hij,jhd->ihd", grad_score, key_heads, preferred_element_type=jnp.float32)
        * scale
    ).reshape(row_count, D)
    key_term = (
        jnp.einsum("hij,ihd->jhd", grad_score, query_heads, preferred_element_type=jnp.float32)
        * scale
    ).reshape(col_count, D)
    value_term = jnp.einsum(
        "hij,ihd->jhd", weights_low, out_heads, preferred_element_type=jnp.float32
    ).reshape(col_count, D)
    query_grad = lax.psum_scatter(query_term, "col", scatter_dimension=1, tiled=True)
    key_grad, value_grad = (
        lax.psum_scatter(key_term, "row", scatter_dimension=1, tiled=True),
        lax.psum_scatter(value_term, "row", scatter_dimension=1, tiled=True),
    )
    return (
        d_pair,
        d_wbias,
        query_grad.astype(jnp.bfloat16),
        key_grad.astype(jnp.bfloat16),
        value_grad.astype(jnp.bfloat16),
    )


def solution(mesh):
    return jax.shard_map(
        on_device,
        mesh=mesh,
        in_specs=(
            P("row", "col", None),
            P(),
            P("row", "col"),
            P("col", "row"),
            P("col", "row"),
            P("row", "col"),
        ),
        out_specs=(P("row", "col", None), P(), P("row", "col"), P("col", "row"), P("col", "row")),
        check_vma=False,
    )
```

profile of v0, /device:TPU:8, one launch (start us, length us, event | category | flops | bytes accessed | tf_op | source)
XLA Modules:
  0.0 433.7 jit_solution(17199849973470065205)
XLA Ops:
  8.9 11.2 %fusion.11 = f32[192,96,96]{2,1,0:T(8,128)} fusion(bf16[192,96,512]{2,1,0:T(8,128)(2,1)} %param.8, bf16[512,96]{0,1:T(8,128)(2,1)S(1)} %copy-done), kind=kOutput, calls=%fused_computation.27 | convolution fusion | flops 1811939328 | bytes 26050560 | tf_op jit(solution)/shard_map/dot_general | solution.py:47
  20.1 12.1 %copy.40 = f32[192,96,96]{0,1,2:T(8,128)} copy(f32[192,96,96]{2,1,0:T(8,128)} %fusion.11) | data formatting | bytes 14155776 | tf_op jit(solution)/shard_map/dot_general | solution.py:47
  32.4 29.7 %all_gather.30 = bf16[192,1536]{0,1:T(8,128)(2,1)S(1)} all-gather(bf16[192,192]{0,1:T(8,128)(2,1)S(1)} %copy.38), channel_id=1, replica_groups=mesh['row'=4,'col'=8] {'col'}, dimensions={1}, use_global_device_ids=true | all-gather | bytes 663552 | tf_op jit(solution)/shard_map/all_gather | solution.py:35
  62.1 5.9 %all_gather.31 = bf16[96,1536]{1,0:T(8,128)(2,1)S(1)} all-gather(bf16[96,384]{1,0:T(8,128)(2,1)S(1)} %copy-done.5), channel_id=1, replica_groups=mesh['row'=4,'col'=8] {'row'}, dimensions={1}, use_global_device_ids=true | all-gather | bytes 368640 | tf_op jit(solution)/shard_map/all_gather | solution.py:39
  68.4 32.2 %all_gather.36 = bf16[192,1536]{0,1:T(8,128)(2,1)S(1)} all-gather(bf16[192,192]{0,1:T(8,128)(2,1)S(1)} %copy.42), channel_id=1, replica_groups=mesh['row'=4,'col'=8] {'col'}, dimensions={1}, use_global_device_ids=true | all-gather | bytes 663552 | tf_op jit(solution)/shard_map/all_gather | solution.py:36
  100.6 5.9 %all_gather.37 = bf16[96,1536]{1,0:T(8,128)(2,1)S(1)} all-gather(bf16[96,384]{1,0:T(8,128)(2,1)S(1)} %copy-done.6), channel_id=1, replica_groups=mesh['row'=4,'col'=8] {'row'}, dimensions={1}, use_global_device_ids=true | all-gather | bytes 368640 | tf_op jit(solution)/shard_map/all_gather | solution.py:40
  106.7 9.2 %fusion.13 = (f32[96,192]{1,0:T(8,128)S(1)}, f32[96,192,96]{1,2,0:T(8,128)S(1)}, f32[96,192,96]{1,2,0:T(8,128)}) fusion(f32[192,96,96]{0,1,2:T(8,128)} %copy.40, bf16[192,96,16]{0,2,1:T(8,128)(2,1)S(1)} %bitcast.92, bf16[96,96,16]{0,2,1:T(8,128)(2,1)S(1)} %bitcast.96), kind=kOutput, calls=%fused_computation.29 | convolution fusion | flops 61913088 | bytes 22192128 | tf_op jit(solution)/shard_map/ihd,jhd->hij/dot_general | solution.py:51
  115.8 5.7 %multiply_reduce_fusion = (f32[96,192]{1,0:T(8,128)S(1)}, f32[96,192]{1,0:T(8,128)S(1)}, f32[96,192,96]{1,2,0:T(8,128)}) fusion(f32[96,192,96]{1,2,0:T(8,128)S(1)} %get-tuple-element.66, f32[96,192]{1,0:T(8,128)S(1)} %get-tuple-element.65, bf16[192,96,16]{0,2,1:T(8,128)(2,1)S(1)} %bitcast.98, bf16[96,96,16]{0,2,1:T(8,128)(2,1)S(1)} %bitcast.103), kind=kOutput, calls=%fused_computation.19 | convolution fusion | flops 63664128 | bytes 15261696 | tf_op jit(solution)/shard_map/ihd,jhd->hij/dot_general | solution.py:54
  122.1 32.1 %all-gather.1 = f32[768,192]{1,0:T(8,128)S(1)} all-gather(f32[96,192]{1,0:T(8,128)S(1)} %get-tuple-element.48), channel_id=3, replica_groups=mesh['row'=4,'col'=8] {'col'}, dimensions={0}, use_global_device_ids=true | all-gather | bytes 663552 | tf_op jit(solution)/shard_map/all_gather | solution.py:13
  155.2 32.1 %all-gather.2 = f32[768,192]{1,0:T(8,128)S(1)} all-gather(f32[96,192]{1,0:T(8,128)S(1)} %get-tuple-element.47), channel_id=4, replica_groups=mesh['row'=4,'col'=8] {'col'}, dimensions={0}, use_global_device_ids=true | all-gather | bytes 663552 | tf_op jit(solution)/shard_map/all_gather | solution.py:13
  188.2 32.0 %all-gather = f32[768,192]{1,0:T(8,128)S(1)} all-gather(f32[96,192]{1,0:T(8,128)S(1)} %get-tuple-element.65), channel_id=2, replica_groups=mesh['row'=4,'col'=8] {'col'}, dimensions={0}, use_global_device_ids=true | all-gather | bytes 663552 | tf_op jit(solution)/shard_map/all_gather | solution.py:13
  220.3 13.8 %while.14 = (s32[]{:T(128)}, f32[96,192]{1,0:T(8,128)S(1)}, f32[96,192]{1,0:T(8,128)S(1)}, f32[96,192]{1,0:T(8,128)S(1)}, f32[7,96,192]{2,1,0:T(8,128)S(1)}, /*i...) while((s32[]{:T(128)}, f32[96,192]{1,0:T(8,128)S(1)}, f32[96,192]{1,0:T(8,128)S(1)}, ...), condition=%wide.region_4.5_spmd, body=%wide.region_3.4_spmd.sunk | while | flops 202754 | bytes 1032285 | solution.py:16
  222.3 1.0 fusion.30
  234.2 6.2 %fusion.9 = f32[96,96,16]{1,2,0:T(8,128)} fusion(bf16[192,96,16]{0,2,1:T(8,128)(2,1)S(1)} %bitcast.99, f32[96,192,96]{1,2,0:T(8,128)} %copy-done.1, f32[96,192]{1,0:T(8,128)S(1)} %get-tuple-element.45, f32[96,192]{1,0:T(8,128)S(1)} %get-tuple-element.44), kind=kOutput, calls=%fused_computation.22 | convolution fusion | flops 61931520 | bytes 8404992 | tf_op jit(solution)/shard_map/hij,ihd->jhd/dot_general | solution.py:85
  240.3 2.2 copy.51
  242.8 7.9 %multiply_convert_fusion = bf16[96,192,96]{1,2,0:T(8,128)(2,1)S(1)} fusion(f32[96,192,96]{1,2,0:T(8,128)} %get-tuple-element.68, f32[96,192]{1,0:T(8,128)S(1)} %div.21, f32[96,192]{1,0:T(8,128)S(1)} %get-tuple-element.45, f32[96,192,96]{1,2,0:T(8,128)} %copy-done.1, f32[96,192]{1,0:T(8,128)S(1)} %get-tuple-element.44), kind=kLoop, calls=%fused_computation.17 | loop fusion | flops 8847360 | bytes 17915904 | tf_op jit(solution)/shard_map/convert_element_type | solution.py:67
  250.7 2.1 copy-done.2
  252.9 1.3 convolution_multiply_fusion.1
  254.2 1.2 copy.49
  255.4 4.2 convolution_multiply_fusion
  259.7 13.1 %fusion.4 = bf16[192,96,96]{0,1,2:T(8,128)(2,1)} fusion(f32[96,192,96]{1,2,0:T(8,128)} %get-tuple-element.68, f32[192,96,96]{0,1,2:T(8,128)} %copy.40, f32[96,192,96]{1,2,0:T(8,128)} %get-tuple-element.67, f32[192,96]{0,1:T(8,128)S(1)} %bitcast.104, f32[192,96]{0,1:T(8,128)S(1)} %bitcast.91, f32[192,96]{0,1:T(8,128)S(1)} %bitcast.90), kind=kLoop, calls=%fused_computation.11 | loop fusion | flops 12386304 | bytes 24993792 | tf_op jit(solution)/shard_map/convert_element_type | solution.py:67
  272.8 7.6 %copy.45 = bf16[192,96,96]{1,2,0:T(8,128)(2,1)} copy(bf16[192,96,96]{0,1,2:T(8,128)(2,1)} %fusion.4) | data formatting | bytes 7077888 | tf_op jit(solution)/shard_map/convert_element_type | solution.py:67
  280.5 11.8 %convolution_bitcast_fusion = f32[512,96]{0,1:T(8,128)} fusion(bf16[192,96,96]{1,2,0:T(8,128)(2,1)} %copy.45, bf16[192,96,512]{2,1,0:T(8,128)(2,1)} %param.8), kind=kOutput, calls=%fused_computation.26 | convolution fusion | flops 1811939328 | bytes 22609920 | tf_op jit(solution)/shard_map/dot_general | solution.py:75
  292.2 6.7 %copy.44 = bf16[192,96,96]{1,0,2:T(8,128)(2,1)} copy(bf16[192,96,96]{0,1,2:T(8,128)(2,1)} %fusion.4) | data formatting | bytes 7077888 | tf_op jit(solution)/shard_map/convert_element_type | solution.py:67
  299.0 9.2 %reshape.49 = bf16[18432,96]{0,1:T(8,128)(2,1)} reshape(bf16[192,96,96]{1,0,2:T(8,128)(2,1)} %copy.44) | data formatting | bytes 7077888 | tf_op jit(solution)/shard_map/reshape | solution.py:69
  308.2 11.5 %convolution_convert_fusion = bf16[18432,512]{1,0:T(8,128)(2,1)} fusion(bf16[18432,96]{0,1:T(8,128)(2,1)} %reshape.49, bf16[512,96]{0,1:T(8,128)(2,1)S(1)} %copy-done), kind=kOutput, calls=%fused_computation.8 | convolution fusion | flops 1821376512 | bytes 22511616 | tf_op jit(solution)/shard_map/dot_general | solution.py:71
  319.7 1.6 convert_element_type.27
  321.3 1.6 convert_element_type.25
  322.8 38.5 %reduce-scatter.10.cloned.1.call-done = f32[192,192]{1,0:T(8,128)} async-done(((f32[1536,192]{1,0:T(8,128)}), f32[192,192]{1,0:T(8,128)}) %reduce-scatter.10.cloned.1.call-update) | async-done | bytes 147472
  361.4 1.7 copy.56
  363.0 61.9 %all-reduce.2.cloned.1.call-done = f32[512,96]{0,1:T(8,128)} async-done(((f32[512,96]{0,1:T(8,128)}), f32[512,96]{0,1:T(8,128)}) %all-reduce.2.cloned.1.call-update) | async-done | bytes 196624 | tf_op jit(solution)/shard_map/psum | solution.py:76
  425.0 1.6 copy.72
  (54 shorter events, 17.1 us)
Async XLA Ops:
  8.0 0.9 copy-start
  8.0 311.7 %reduce-scatter.8.cloned.1.call-start = ((), (), s32[]{:S(2)}) async-start(), calls=%async_computation.5 | async-start | bytes 737280 | tf_op jit(solution)/shard_map/reduce_scatter | solution.py:91
  20.1 12.2 %copy-start.3 = (bf16[192,192]{1,0:T(8,128)(2,1)S(1)}, bf16[192,192]{1,0:T(8,128)(2,1)}, u32[]{:S(2)}) copy-start(bf16[192,192]{1,0:T(8,128)(2,1)} %param.10) | copy-start | bytes 221188
  20.1 42.0 %copy-start.5 = (bf16[96,384]{1,0:T(8,128)(2,1)S(1)}, bf16[96,384]{1,0:T(8,128)(2,1)}, u32[]{:S(2)}) copy-start(bf16[96,384]{1,0:T(8,128)(2,1)} %param.11) | copy-start | bytes 221188
  20.1 48.1 %copy-start.4 = (bf16[192,192]{1,0:T(8,128)(2,1)S(1)}, bf16[192,192]{1,0:T(8,128)(2,1)}, u32[]{:S(2)}) copy-start(bf16[192,192]{1,0:T(8,128)(2,1)} %param.13) | copy-start | bytes 221188
  20.1 80.5 %copy-start.6 = (bf16[96,384]{1,0:T(8,128)(2,1)S(1)}, bf16[96,384]{1,0:T(8,128)(2,1)}, u32[]{:S(2)}) copy-start(bf16[96,384]{1,0:T(8,128)(2,1)} %param.12) | copy-start | bytes 221188
  115.8 6.3 %copy-start.1 = (f32[96,192,96]{1,2,0:T(8,128)}, f32[96,192,96]{1,2,0:T(8,128)S(1)}, u32[]{:S(2)}) copy-start(f32[96,192,96]{1,2,0:T(8,128)S(1)} %get-tuple-element.66) | copy-start | bytes 21233668
  242.6 78.7 %reduce-scatter.6.cloned.1.call-start = ((), (), s32[]{:S(2)}) async-start(), calls=%async_computation.4 | async-start | bytes 737280 | tf_op jit(solution)/shard_map/reduce_scatter | solution.py:90
  250.7 2.2 copy-start.2
  255.4 106.0 %reduce-scatter.10.cloned.1.call-start = ((), (), s32[]{:S(2)}) async-start(), calls=%async_computation.6 | async-start | bytes 1769472
  259.7 165.3 %all-reduce.2.cloned.1.call-start = ((), (), s32[]{:S(2)}) async-start(), calls=%async_computation.3 | async-start | bytes 393216 | tf_op jit(solution)/shard_map/psum | solution.py:76
Sparse Core Ops, SparseCore 0:
  242.7 25.4 reduce-scatter.7
  270.7 22.0 reduce-scatter.5
  296.2 65.0 reduce-scatter.9
Sparse Core Ops, SparseCore 1:
  292.3 132.6 all-reduce.1
where the time goes:
time: 435 us; the launch traced here: 434 us
  blocking collectives  170 us (39%)
  waiting for transfers between devices  101 us (23%)
  matrix products  61.1 us (14%)
  local copies, waits for them, and re-layouts  48.6 us (11%)
  other arithmetic  37.7 us (9%)
  between operations  15.3 us (4%)
    all_gather x3, blocking collectives, joined(): pieces = jax.tree.map(lambda part: lax.all_gather(part, axis), value)  96.3 us
    psum x1, waiting for transfers between devices, on_device(): d_wbias = lax.psum(weight_term, ('row', 'col'))  61.9 us
    unnamed x5, waiting for transfers between devices  38.6 us
    all_gather x1, blocking collectives, on_device(): lax.all_gather(d_out, 'col', axis=1, tiled=True)  32.2 us
    all_gather x1, blocking collectives, on_device(): lax.all_gather(queries, 'col', axis=1, tiled=True)  29.7 us
    convert_element_type x2, other arithmetic, on_device(): (weights * (grad_prob - row_delta[..., None])).astype(jnp.bfloat16)  21 us
    convert_element_type x2, local copies, waits for them, and re-layouts, on_device(): (weights * (grad_prob - row_delta[..., None])).astype(jnp.bfloat16)  14.4 us
    dot_general x1, local copies, waits for them, and re-layouts, on_device(): jnp.dot(flat_pair, w_bias, preferred_element_type=jnp.float32)  12.1 us
  transfers between devices with their start and end apart: 4, of which 2 were waited for; matrix products, arithmetic and copies ran while one was open for 18% of the time, Pallas kernels for 0%

commit v1 on v0

--- a/solution.py
+++ b/solution.py
@@ -73,7 +73,7 @@
         .reshape(row_count, col_count, P_SIZE)
     )
     weight_term = jnp.dot(flat_pair.T, score_flat, preferred_element_type=jnp.float32)
-    d_wbias = lax.psum(weight_term, ("row", "col"))
+    d_wbias = jnp.sum(lax.all_gather(weight_term, ("row", "col")), axis=0)
     query_term = (
         jnp.einsum("hij,jhd->ihd", grad_score, key_heads, preferred_element_type=jnp.float32)
         * scale

time: 435 us -> 392 us (0.901)
  waiting for transfers between devices: 101 us -> 48.8 us
  local copies, waits for them, and re-layouts: 48.6 us -> 54.1 us
    psum x1 -> x0, waiting for transfers between devices: 61.9 us -> none  [on_device(): d_wbias = lax.psum(weight_term, ('row', 'col'))]
    unnamed x5, waiting for transfers between devices: 38.6 us -> 48.8 us
    unnamed x18, local copies, waits for them, and re-layouts: 7.11 us -> 12.6 us
  transfers between devices with their start and end apart: 4 -> 4, of which waited for: 2 -> 1; matrix products, arithmetic and copies ran while one was open for 18% -> 20% of each run, Pallas kernels for 0% -> 0%
where the time goes in v1:
time: 392 us; the launch traced here: 389 us
  blocking collectives  170 us (43%)
  matrix products  61.1 us (16%)
  local copies, waits for them, and re-layouts  54.1 us (14%)
  waiting for transfers between devices  48.8 us (12%)
  other arithmetic  39.5 us (10%)
  between operations  15.3 us (4%)
    all_gather x3, blocking collectives, joined(): pieces = jax.tree.map(lambda part: lax.all_gather(part, axis), value)  96.3 us
    unnamed x5, waiting for transfers between devices  48.8 us
    all_gather x1, blocking collectives, on_device(): lax.all_gather(d_out, 'col', axis=1, tiled=True)  32.2 us
    all_gather x1, blocking collectives, on_device(): lax.all_gather(queries, 'col', axis=1, tiled=True)  29.7 us
    convert_element_type x2, other arithmetic, on_device(): (weights * (grad_prob - row_delta[..., None])).astype(jnp.bfloat16)  21 us
    convert_element_type x2, local copies, waits for them, and re-layouts, on_device(): (weights * (grad_prob - row_delta[..., None])).astype(jnp.bfloat16)  14.4 us
    unnamed x18, local copies, waits for them, and re-layouts  12.6 us
    dot_general x1, local copies, waits for them, and re-layouts, on_device(): jnp.dot(flat_pair, w_bias, preferred_element_type=jnp.float32)  12.1 us
  transfers between devices with their start and end apart: 4, of which 1 were waited for; matrix products, arithmetic and copies ran while one was open for 20% of the time, Pallas kernels for 0%

profile of v1, /device:TPU:8, one launch (start us, length us, event | category | flops | bytes accessed | tf_op | source)
XLA Modules:
  0.0 389.4 jit_solution(12814721808830343179)
XLA Ops:
  8.9 11.2 %fusion.11 = f32[192,96,96]{2,1,0:T(8,128)} fusion(bf16[192,96,512]{2,1,0:T(8,128)(2,1)} %param.8, bf16[512,96]{0,1:T(8,128)(2,1)S(1)} %copy-done), kind=kOutput, calls=%fused_computation.28 | convolution fusion | flops 1811939328 | bytes 26050560 | tf_op jit(solution)/shard_map/dot_general | solution.py:47
  20.1 12.1 %copy.40 = f32[192,96,96]{0,1,2:T(8,128)} copy(f32[192,96,96]{2,1,0:T(8,128)} %fusion.11) | data formatting | bytes 14155776 | tf_op jit(solution)/shard_map/dot_general | solution.py:47
  32.4 29.7 %all_gather.36 = bf16[192,1536]{0,1:T(8,128)(2,1)S(1)} all-gather(bf16[192,192]{0,1:T(8,128)(2,1)S(1)} %copy.38), channel_id=1, replica_groups=mesh['row'=4,'col'=8] {'col'}, dimensions={1}, use_global_device_ids=true | all-gather | bytes 663552 | tf_op jit(solution)/shard_map/all_gather | solution.py:35
  62.1 5.9 %all_gather.37 = bf16[96,1536]{1,0:T(8,128)(2,1)S(1)} all-gather(bf16[96,384]{1,0:T(8,128)(2,1)S(1)} %copy-done.5), channel_id=1, replica_groups=mesh['row'=4,'col'=8] {'row'}, dimensions={1}, use_global_device_ids=true | all-gather | bytes 368640 | tf_op jit(solution)/shard_map/all_gather | solution.py:39
  68.4 32.2 %all_gather.42 = bf16[192,1536]{0,1:T(8,128)(2,1)S(1)} all-gather(bf16[192,192]{0,1:T(8,128)(2,1)S(1)} %copy.42), channel_id=1, replica_groups=mesh['row'=4,'col'=8] {'col'}, dimensions={1}, use_global_device_ids=true | all-gather | bytes 663552 | tf_op jit(solution)/shard_map/all_gather | solution.py:36
  100.6 5.9 %all_gather.43 = bf16[96,1536]{1,0:T(8,128)(2,1)S(1)} all-gather(bf16[96,384]{1,0:T(8,128)(2,1)S(1)} %copy-done.6), channel_id=1, replica_groups=mesh['row'=4,'col'=8] {'row'}, dimensions={1}, use_global_device_ids=true | all-gather | bytes 368640 | tf_op jit(solution)/shard_map/all_gather | solution.py:40
  106.7 9.2 %fusion.13 = (f32[96,192]{1,0:T(8,128)S(1)}, f32[96,192,96]{1,2,0:T(8,128)S(1)}, f32[96,192,96]{1,2,0:T(8,128)}) fusion(f32[192,96,96]{0,1,2:T(8,128)} %copy.40, bf16[192,96,16]{0,2,1:T(8,128)(2,1)S(1)} %bitcast.97, bf16[96,96,16]{0,2,1:T(8,128)(2,1)S(1)} %bitcast.102), kind=kOutput, calls=%fused_computation.30 | convolution fusion | flops 61913088 | bytes 22192128 | tf_op jit(solution)/shard_map/ihd,jhd->hij/dot_general | solution.py:51
  115.8 5.7 %multiply_reduce_fusion = (f32[96,192]{1,0:T(8,128)S(1)}, f32[96,192]{1,0:T(8,128)S(1)}, f32[96,192,96]{1,2,0:T(8,128)}) fusion(f32[96,192,96]{1,2,0:T(8,128)S(1)} %get-tuple-element.66, f32[96,192]{1,0:T(8,128)S(1)} %get-tuple-element.65, bf16[192,96,16]{0,2,1:T(8,128)(2,1)S(1)} %bitcast.104, bf16[96,96,16]{0,2,1:T(8,128)(2,1)S(1)} %bitcast.109), kind=kOutput, calls=%fused_computation.19 | convolution fusion | flops 63664128 | bytes 15261696 | tf_op jit(solution)/shard_map/ihd,jhd->hij/dot_general | solution.py:54
  122.1 32.1 %all-gather.1 = f32[768,192]{1,0:T(8,128)S(1)} all-gather(f32[96,192]{1,0:T(8,128)S(1)} %get-tuple-element.48), channel_id=3, replica_groups=mesh['row'=4,'col'=8] {'col'}, dimensions={0}, use_global_device_ids=true | all-gather | bytes 663552 | tf_op jit(solution)/shard_map/all_gather | solution.py:13
  155.2 32.1 %all-gather.2 = f32[768,192]{1,0:T(8,128)S(1)} all-gather(f32[96,192]{1,0:T(8,128)S(1)} %get-tuple-element.47), channel_id=4, replica_groups=mesh['row'=4,'col'=8] {'col'}, dimensions={0}, use_global_device_ids=true | all-gather | bytes 663552 | tf_op jit(solution)/shard_map/all_gather | solution.py:13
  188.2 32.0 %all-gather = f32[768,192]{1,0:T(8,128)S(1)} all-gather(f32[96,192]{1,0:T(8,128)S(1)} %get-tuple-element.65), channel_id=2, replica_groups=mesh['row'=4,'col'=8] {'col'}, dimensions={0}, use_global_device_ids=true | all-gather | bytes 663552 | tf_op jit(solution)/shard_map/all_gather | solution.py:13
  220.3 13.8 %while.14 = (s32[]{:T(128)}, f32[96,192]{1,0:T(8,128)S(1)}, f32[96,192]{1,0:T(8,128)S(1)}, f32[96,192]{1,0:T(8,128)S(1)}, f32[7,96,192]{2,1,0:T(8,128)S(1)}, /*i...) while((s32[]{:T(128)}, f32[96,192]{1,0:T(8,128)S(1)}, f32[96,192]{1,0:T(8,128)S(1)}, ...), condition=%wide.region_4.5_spmd, body=%wide.region_3.4_spmd.sunk | while | flops 202754 | bytes 1032285 | solution.py:16
  222.3 1.0 fusion.30
  234.2 6.2 %fusion.9 = f32[96,96,16]{1,2,0:T(8,128)} fusion(bf16[192,96,16]{0,2,1:T(8,128)(2,1)S(1)} %bitcast.105, f32[96,192,96]{1,2,0:T(8,128)} %copy-done.1, f32[96,192]{1,0:T(8,128)S(1)} %get-tuple-element.45, f32[96,192]{1,0:T(8,128)S(1)} %get-tuple-element.44), kind=kOutput, calls=%fused_computation.23 | convolution fusion | flops 61931520 | bytes 8404992 | tf_op jit(solution)/shard_map/hij,ihd->jhd/dot_general | solution.py:85
  240.3 2.2 copy.51
  242.8 7.9 %multiply_convert_fusion = bf16[96,192,96]{1,2,0:T(8,128)(2,1)S(1)} fusion(f32[96,192,96]{1,2,0:T(8,128)} %get-tuple-element.68, f32[96,192]{1,0:T(8,128)S(1)} %div.21, f32[96,192]{1,0:T(8,128)S(1)} %get-tuple-element.45, f32[96,192,96]{1,2,0:T(8,128)} %copy-done.1, f32[96,192]{1,0:T(8,128)S(1)} %get-tuple-element.44), kind=kLoop, calls=%fused_computation.17 | loop fusion | flops 8847360 | bytes 17915904 | tf_op jit(solution)/shard_map/convert_element_type | solution.py:67
  250.7 2.1 copy-done.2
  252.9 1.3 convolution_multiply_fusion.1
  254.2 1.2 copy.49
  255.4 4.2 %convolution_multiply_fusion = f32[96,192,16]{1,2,0:T(8,128)} fusion(bf16[96,96,16]{0,2,1:T(8,128)(2,1)S(1)} %bitcast.103, bf16[96,192,96]{1,2,0:T(8,128)(2,1)} %copy-done.2), kind=kOutput, calls=%fused_computation.25 | convolution fusion | flops 56918016 | bytes 5013504 | tf_op jit(solution)/shard_map/hij,jhd->ihd/dot_general | solution.py:78
  259.7 13.1 %fusion.4 = bf16[192,96,96]{0,1,2:T(8,128)(2,1)} fusion(f32[96,192,96]{1,2,0:T(8,128)} %get-tuple-element.68, f32[192,96,96]{0,1,2:T(8,128)} %copy.40, f32[96,192,96]{1,2,0:T(8,128)} %get-tuple-element.67, f32[192,96]{0,1:T(8,128)S(1)} %bitcast.110, f32[192,96]{0,1:T(8,128)S(1)} %bitcast.96, f32[192,96]{0,1:T(8,128)S(1)} %bitcast.95), kind=kLoop, calls=%fused_computation.11 | loop fusion | flops 12386304 | bytes 24993792 | tf_op jit(solution)/shard_map/convert_element_type | solution.py:67
  272.8 7.6 %copy.45 = bf16[192,96,96]{1,2,0:T(8,128)(2,1)} copy(bf16[192,96,96]{0,1,2:T(8,128)(2,1)} %fusion.4) | data formatting | bytes 7077888 | tf_op jit(solution)/shard_map/convert_element_type | solution.py:67
  280.5 11.8 %convolution_bitcast_fusion = f32[512,96]{0,1:T(8,128)} fusion(bf16[192,96,96]{1,2,0:T(8,128)(2,1)} %copy.45, bf16[192,96,512]{2,1,0:T(8,128)(2,1)} %param.8), kind=kOutput, calls=%fused_computation.27 | convolution fusion | flops 1811939328 | bytes 22609920 | tf_op jit(solution)/shard_map/dot_general | solution.py:75
  292.2 6.7 %copy.44 = bf16[192,96,96]{1,0,2:T(8,128)(2,1)} copy(bf16[192,96,96]{0,1,2:T(8,128)(2,1)} %fusion.4) | data formatting | bytes 7077888 | tf_op jit(solution)/shard_map/convert_element_type | solution.py:67
  299.0 9.2 %reshape.49 = bf16[18432,96]{0,1:T(8,128)(2,1)} reshape(bf16[192,96,96]{1,0,2:T(8,128)(2,1)} %copy.44) | data formatting | bytes 7077888 | tf_op jit(solution)/shard_map/reshape | solution.py:69
  308.2 11.5 %convolution_convert_fusion = bf16[18432,512]{1,0:T(8,128)(2,1)} fusion(bf16[18432,96]{0,1:T(8,128)(2,1)} %reshape.49, bf16[512,96]{0,1:T(8,128)(2,1)S(1)} %copy-done), kind=kOutput, calls=%fused_computation.8 | convolution fusion | flops 1821376512 | bytes 22511616 | tf_op jit(solution)/shard_map/dot_general | solution.py:71
  319.8 1.6 convert_element_type.27
  321.3 1.6 convert_element_type.25
  322.9 48.8 %reduce-scatter.10.cloned.1.call-done = f32[192,192]{1,0:T(8,128)} async-done(((f32[1536,192]{1,0:T(8,128)}), f32[192,192]{1,0:T(8,128)}) %reduce-scatter.10.cloned.1.call-update) | async-done | bytes 147472
  371.6 1.7 copy.56
  373.3 7.1 %copy.57 = f32[12,8,32,512]{3,2,1,0:T(8,128)S(1)} copy(f32[12,8,32,512]{3,1,2,0:T(8,128)} %bitcast.99) | data formatting | bytes 12582912
  380.4 1.8 bitcast_reduce_fusion
  (55 shorter events, 17.1 us)
Async XLA Ops:
  8.0 0.9 copy-start
  8.0 311.7 %reduce-scatter.8.cloned.1.call-start = ((), (), s32[]{:S(2)}) async-start(), calls=%async_computation.4 | async-start | bytes 737280 | tf_op jit(solution)/shard_map/reduce_scatter | solution.py:91
  20.1 12.2 %copy-start.3 = (bf16[192,192]{1,0:T(8,128)(2,1)S(1)}, bf16[192,192]{1,0:T(8,128)(2,1)}, u32[]{:S(2)}) copy-start(bf16[192,192]{1,0:T(8,128)(2,1)} %param.10) | copy-start | bytes 221188
  20.1 42.0 %copy-start.5 = (bf16[96,384]{1,0:T(8,128)(2,1)S(1)}, bf16[96,384]{1,0:T(8,128)(2,1)}, u32[]{:S(2)}) copy-start(bf16[96,384]{1,0:T(8,128)(2,1)} %param.11) | copy-start | bytes 221188
  20.1 48.1 %copy-start.4 = (bf16[192,192]{1,0:T(8,128)(2,1)S(1)}, bf16[192,192]{1,0:T(8,128)(2,1)}, u32[]{:S(2)}) copy-start(bf16[192,192]{1,0:T(8,128)(2,1)} %param.13) | copy-start | bytes 221188
  20.1 80.5 %copy-start.6 = (bf16[96,384]{1,0:T(8,128)(2,1)S(1)}, bf16[96,384]{1,0:T(8,128)(2,1)}, u32[]{:S(2)}) copy-start(bf16[96,384]{1,0:T(8,128)(2,1)} %param.12) | copy-start | bytes 221188
  115.8 6.3 %copy-start.1 = (f32[96,192,96]{1,2,0:T(8,128)}, f32[96,192,96]{1,2,0:T(8,128)S(1)}, u32[]{:S(2)}) copy-start(f32[96,192,96]{1,2,0:T(8,128)S(1)} %get-tuple-element.66) | copy-start | bytes 21233668
  242.6 78.7 %reduce-scatter.6.cloned.1.call-start = ((), (), s32[]{:S(2)}) async-start(), calls=%async_computation.3 | async-start | bytes 737280 | tf_op jit(solution)/shard_map/reduce_scatter | solution.py:90
  250.7 2.2 copy-start.2
  255.4 116.3 %reduce-scatter.10.cloned.1.call-start = ((), (), s32[]{:S(2)}) async-start(), calls=%async_computation.6 | async-start | bytes 1769472
  259.7 113.6 %all-gather.6.cloned.1.call-start = ((), (), s32[]{:S(2)}) async-start(), calls=%async_computation.5 | async-start | bytes 6488064 | tf_op jit(solution)/shard_map/all_gather | solution.py:76
Sparse Core Ops, SparseCore 0:
  242.7 25.4 reduce-scatter.7
  270.7 22.0 reduce-scatter.5
  296.2 75.3 reduce-scatter.9
Sparse Core Ops, SparseCore 1:
  292.3 77.8 all-gather.5
